TPU v7x, 32 devices: a whole 2x2x4 slice. The times are simulated.
32 devices in a mesh: dp: 8 (over y, x, core), tensor: 4 (over z).
Axes of the slice: x: 2, y: 2, z: 4, core: 2. Of those that a mesh axis runs over, the one named last changes fastest.
Arguments:
- latents: bfloat16 [16384, 1280], P('dp'), may hold values from -6 to 6
- norm1_gain: float32 [1280], replicated, may hold values from 0.5 to 1.5
- norm1_shift: float32 [1280], replicated, may hold values from -1.75 to 1.75
- query_weight: bfloat16 [1280, 1280], P(None, 'tensor'), may hold values from -0.15625 to 0.15625
- query_bias: float32 [1280], P('tensor'), may hold values from -1.75 to 1.75
- key_weight: bfloat16 [1280, 1280], P(None, 'tensor'), may hold values from -0.15625 to 0.15625
- value_weight: bfloat16 [1280, 1280], P(None, 'tensor'), may hold values from -0.15625 to 0.15625
- value_bias: float32 [1280], P('tensor'), may hold values from -1.75 to 1.75
- out_weight: bfloat16 [1280, 1280], P('tensor'), may hold values from -0.625 to 0.625
- out_bias: float32 [1280], replicated, may hold values from -1.75 to 1.75
- norm2_gain: float32 [1280], replicated, may hold values from 0.5 to 1.5
- norm2_shift: float32 [1280], replicated, may hold values from -1.75 to 1.75
- hidden_weight: bfloat16 [1280, 1280], P(None, 'tensor'), may hold values from -0.15625 to 0.15625
- hidden_bias: float32 [1280], P('tensor'), may hold values from -1.75 to 1.75
- proj_weight: bfloat16 [1280, 1280], P('tensor'), may hold values from -0.25 to 0.25
- proj_bias: float32 [1280], replicated, may hold values from -1.75 to 1.75
- segments: int32 [16, 1024], P('dp'), may hold values from 0 to 7, never falling along the last dimension, each value on 1 to 512 neighbouring positions
- valid_mask: int32 [16, 1024], P('dp'), may hold values 0 or 1
- cotangent: bfloat16 [16384, 1280], P('dp'), may hold values from -6 to 6
Outputs:
- output: bfloat16 [16384, 1280], P('dp')
- grad_input: float32 [16384, 1280], P('dp')
- grad_norm1_gain: float32 [1280], replicated
- grad_norm1_shift: float32 [1280], replicated
- grad_query_weight: float32 [1280, 1280], P(None, 'tensor')
- grad_query_bias: float32 [1280], P('tensor')
- grad_key_weight: float32 [1280, 1280], P(None, 'tensor')
- grad_value_weight: float32 [1280, 1280], P(None, 'tensor')
- grad_value_bias: float32 [1280], P('tensor')
- grad_out_weight: float32 [1280, 1280], P('tensor')
- grad_out_bias: float32 [1280], replicated
- grad_norm2_gain: float32 [1280], replicated
- grad_norm2_shift: float32 [1280], replicated
- grad_hidden_weight: float32 [1280, 1280], P(None, 'tensor')
- grad_hidden_bias: float32 [1280], P('tensor')
- grad_proj_weight: float32 [1280, 1280], P('tensor')
- grad_proj_bias: float32 [1280], replicated
- rms: float32 [16, 3], P('dp')
Inputs may be any that keep to these rules, and one draw needn't show every extreme that they name: `segments`: in each row segment numbers never fall, each document has 1 to 512 positions, and one has exactly that many.
All inputs are finite; a program needn't handle non-finite values. No bound on the sum of `valid_mask` on one device may be relied on, other than what follows from the above.
Results may differ from a plain program's by a relative error of at most 0.013.
Values sent between devices are 32-bit elements; how exact they have to be, the bound alone decides.
A program may use at most 192 MiB of HBM per device.

v0:
```python
import math
import jax
import jax.numpy as jnp
from jax import lax
from jax.sharding import PartitionSpec as P

HEAD_DIM = 160
EPS = 1e-05
NEG = -1e30


def layer_norm(v, gain, shift):
    center = v - jnp.mean(v, axis=-1, keepdims=True)
    spread = jnp.mean(center * center, axis=-1, keepdims=True)
    return center * lax.rsqrt(spread + EPS) * gain + shift


def inner(left, right):
    return lax.dot_general(
        left, right, (((0,), (0,)), ((), ())), preferred_element_type=jnp.float32
    )


def outer(left, right):
    return lax.dot_general(
        left, right, (((1,), (1,)), ((), ())), preferred_element_type=jnp.float32
    )


def mask_of(seg):
    length = seg.shape[0]
    rowpos = lax.broadcasted_iota(jnp.int32, (length, length), 0)
    colpos = lax.broadcasted_iota(jnp.int32, (length, length), 1)
    return ((rowpos >= colpos) & (seg[:, None] == seg[None, :]))[None]


def scores_of(query, keyed, seg):
    scores = jnp.einsum(
        "qhe,khe->hqk", query, keyed, preferred_element_type=jnp.float32
    ) / math.sqrt(HEAD_DIM)
    allowed = mask_of(seg)
    return (jnp.where(allowed, scores, NEG), allowed)


def attend_forward(query, keyed, valued, seg):
    scores, allowed = scores_of(query, keyed, seg)
    top = jnp.max(scores, axis=-1, keepdims=True)
    weights = jnp.where(allowed, jnp.exp(scores - top), 0.0)
    total = jnp.sum(weights, axis=-1, keepdims=True)
    probs = (weights / total).astype(jnp.bfloat16)
    mixed = jnp.einsum("hqk,khe->qhe", probs, valued, preferred_element_type=jnp.float32).astype(
        jnp.bfloat16
    )
    return (mixed, (top + jnp.log(total))[..., 0])


def attend_backward(query, keyed, valued, seg, logsum, d_mixed):
    scores, allowed = scores_of(query, keyed, seg)
    probs = jnp.where(allowed, jnp.exp(scores - logsum[..., None]), 0.0)
    low_probs = probs.astype(jnp.bfloat16)
    d_valued = jnp.einsum(
        "hqk,qhe->khe", low_probs, d_mixed, preferred_element_type=jnp.float32
    ).astype(jnp.bfloat16)
    d_probs = jnp.einsum("qhe,khe->hqk", d_mixed, valued, preferred_element_type=jnp.float32)
    d_scores = probs * (d_probs - jnp.sum(probs * d_probs, axis=-1, keepdims=True))
    low_scores = d_scores.astype(jnp.bfloat16)
    scale = 1.0 / math.sqrt(HEAD_DIM)
    d_query = (
        jnp.einsum("hqk,khe->qhe", low_scores, keyed, preferred_element_type=jnp.float32) * scale
    ).astype(jnp.bfloat16)
    d_keyed = (
        jnp.einsum("hqk,qhe->khe", low_scores, query, preferred_element_type=jnp.float32) * scale
    ).astype(jnp.bfloat16)
    return (d_query, d_keyed, d_valued)


def shards(
    latents,
    norm1_gain,
    norm1_shift,
    query_weight,
    query_bias,
    key_weight,
    value_weight,
    value_bias,
    out_weight,
    out_bias,
    norm2_gain,
    norm2_shift,
    hidden_weight,
    hidden_bias,
    proj_weight,
    proj_bias,
    segments,
    valid_mask,
    cotangent,
):
    seq_count, length = segments.shape
    tok_rows, width = latents.shape
    local_heads = query_weight.shape[1] // HEAD_DIM

    def split(t):
        return t.reshape(seq_count, length, local_heads, HEAD_DIM)

    inputs = latents.astype(jnp.float32)
    normed1 = layer_norm(inputs, norm1_gain, norm1_shift).astype(jnp.bfloat16)
    query = (
        jnp.dot(normed1, query_weight, preferred_element_type=jnp.float32) + query_bias
    ).astype(jnp.bfloat16)
    keyed = jnp.dot(normed1, key_weight, preferred_element_type=jnp.float32).astype(jnp.bfloat16)
    valued = (
        jnp.dot(normed1, value_weight, preferred_element_type=jnp.float32) + value_bias
    ).astype(jnp.bfloat16)
    mixed, logsum = lax.map(
        lambda t: attend_forward(t[0], t[1], t[2], t[3]),
        (split(query), split(keyed), split(valued), segments),
    )
    mixed = mixed.reshape(tok_rows, local_heads * HEAD_DIM)
    attended = (
        lax.psum(jnp.dot(mixed, out_weight, preferred_element_type=jnp.float32), "tensor")
        + out_bias
    )
    resid = inputs + attended
    normed2 = layer_norm(resid, norm2_gain, norm2_shift).astype(jnp.bfloat16)
    pre = jnp.dot(normed2, hidden_weight, preferred_element_type=jnp.float32) + hidden_bias
    act = jax.nn.gelu(pre, approximate=False).astype(jnp.bfloat16)
    branch = (
        lax.psum(jnp.dot(act, proj_weight, preferred_element_type=jnp.float32), "tensor")
        + proj_bias
    )
    output = resid + branch
    weight = valid_mask.astype(jnp.float32)
    counted = jnp.maximum(jnp.sum(weight, axis=1), 1.0) * width

    def per_seq(v):
        return jnp.sum(weight * jnp.sum(v * v, axis=-1).reshape(seq_count, length), axis=1)

    stat_sums = jnp.stack([per_seq(attended), per_seq(branch), per_seq(output)], axis=1)
    rms = jnp.sqrt(stat_sums / counted[:, None])
    grad_out = cotangent.astype(jnp.float32)
    grad_w2 = inner(act, cotangent)
    grad_b2 = jnp.sum(grad_out, axis=0)
    d_act = outer(cotangent, proj_weight)
    d_pre = jax.vjp(lambda t: jax.nn.gelu(t, approximate=False), pre)[1](d_act)[0]
    low_pre = d_pre.astype(jnp.bfloat16)
    grad_w1 = inner(normed2, low_pre)
    grad_b1 = jnp.sum(low_pre.astype(jnp.float32), axis=0)
    d_normed2 = lax.psum(outer(low_pre, hidden_weight), "tensor")
    norm_back2 = jax.vjp(layer_norm, resid, norm2_gain, norm2_shift)[1]
    d_resid_norm, grad_g2, grad_c2 = norm_back2(d_normed2)
    d_resid = grad_out + d_resid_norm
    low_attended = d_resid.astype(jnp.bfloat16)
    grad_bo = jnp.sum(low_attended.astype(jnp.float32), axis=0)
    grad_wo = inner(mixed, low_attended)
    d_mixed = outer(low_attended, out_weight).astype(jnp.bfloat16)
    d_query, d_keyed, d_valued = lax.map(
        lambda t: attend_backward(t[0], t[1], t[2], t[3], t[4], t[5]),
        (split(query), split(keyed), split(valued), segments, logsum, split(d_mixed)),
    )
    d_query = d_query.reshape(tok_rows, local_heads * HEAD_DIM)
    d_keyed = d_keyed.reshape(tok_rows, local_heads * HEAD_DIM)
    d_valued = d_valued.reshape(tok_rows, local_heads * HEAD_DIM)
    grad_wq = inner(normed1, d_query)
    grad_bq = jnp.sum(d_query.astype(jnp.float32), axis=0)
    grad_wk = inner(normed1, d_keyed)
    grad_wv = inner(normed1, d_valued)
    grad_bv = jnp.sum(d_valued.astype(jnp.float32), axis=0)
    partial_in = (
        outer(d_query, query_weight) + outer(d_keyed, key_weight) + outer(d_valued, value_weight)
    )
    d_normed1 = lax.psum(partial_in, "tensor")
    norm_back1 = jax.vjp(layer_norm, inputs, norm1_gain, norm1_shift)[1]
    d_input_norm, grad_g1, grad_c1 = norm_back1(d_normed1)
    grad_input = d_resid + d_input_norm
    (
        grad_g1,
        grad_c1,
        grad_wq,
        grad_bq,
        grad_wk,
        grad_wv,
        grad_bv,
        grad_wo,
        grad_bo,
        grad_g2,
        grad_c2,
        grad_w1,
        grad_b1,
        grad_w2,
        grad_b2,
    ) = lax.psum(
        (
            grad_g1,
            grad_c1,
            grad_wq,
            grad_bq,
            grad_wk,
            grad_wv,
            grad_bv,
            grad_wo,
            grad_bo,
            grad_g2,
            grad_c2,
            grad_w1,
            grad_b1,
            grad_w2,
            grad_b2,
        ),
        "dp",
    )
    return (
        output.astype(jnp.bfloat16),
        grad_input,
        grad_g1,
        grad_c1,
        grad_wq,
        grad_bq,
        grad_wk,
        grad_wv,
        grad_bv,
        grad_wo,
        grad_bo,
        grad_g2,
        grad_c2,
        grad_w1,
        grad_b1,
        grad_w2,
        grad_b2,
        rms,
    )


def solution(mesh):
    placed = (
        P("dp", None),
        P(),
        P(),
        P(None, "tensor"),
        P("tensor"),
        P(None, "tensor"),
        P(None, "tensor"),
        P("tensor"),
        P("tensor", None),
        P(),
        P(),
        P(),
        P(None, "tensor"),
        P("tensor"),
        P("tensor", None),
        P(),
        P("dp", None),
        P("dp", None),
        P("dp", None),
    )
    return jax.shard_map(
        shards,
        mesh=mesh,
        in_specs=placed,
        out_specs=(
            P("dp", None),
            P("dp", None),
            P(),
            P(),
            P(None, "tensor"),
            P("tensor"),
            P(None, "tensor"),
            P(None, "tensor"),
            P("tensor"),
            P("tensor", None),
            P(),
            P(),
            P(),
            P(None, "tensor"),
            P("tensor"),
            P("tensor", None),
            P(),
            P("dp", None),
        ),
        check_vma=False,
    )
```

profile of v0, /device:TPU:0, one launch (start us, length us, event | category | flops | bytes accessed | tf_op | source)
XLA Modules:
  0.0 1821.8 jit_solution(10788580656488504458)
XLA Ops:
  41.4 20.8 %while.26 = (s32[]{:T(128)}, bf16[2,1024,2,160]{1,3,2,0:T(8,128)(2,1)}, f32[2,2,1024]{2,1,0:T(2,128)S(1)}, bf16[2,1024,2,160]{1,3,2,0:T(8,128)(2,1)S(1)}, s32[2,...) while((s32[]{:T(128)}, ...), condition=%wide.region_5.6_spmd, body=%wide.region_2.5_spmd.sunk | while | flops 1375008768 | bytes 42547356 | solution.py:114
  73.5 360.7 %all-reduce.8.cloned.1.call-done = f32[2048,1280]{1,0:T(8,128)} async-done(((f32[2048,1280]{1,0:T(8,128)}), f32[2048,1280]{1,0:T(8,128)}) %all-reduce.8.cloned.1.call-update) | async-done | bytes 10485776 | tf_op jit(solution)/shard_map/psum | solution.py:120
  434.3 11.8 fusion.86
  459.3 10.2 convert_reduce_fusion.3
  481.3 697.6 %all-reduce.14.cloned.1.call-done = (f32[2048,1280]{1,0:T(8,128)}, f32[2048,1280]{1,0:T(8,128)}) async-done(((f32[2048,1280]{1,0:T(8,128)}, f32[2048,1280]{1,0:T(8,128)}), (f32[2048,1280]{1,0:T(8,128)}, f32[2048,1280]{1,0:T(8,128)})) %all-reduce.14.cloned.1.call-update) | async-done | bytes 20971536 | tf_op jit(solution)/shard_map/psum | solution.py:128
  1179.0 15.7 multiply_reduce_fusion.2
  1200.9 7.7 convert_reduce_fusion.2
  1220.0 55.4 %while.27 = (s32[]{:T(128)}, bf16[2,1024,2,160]{1,3,2,0:T(8,128)(2,1)}, bf16[2,1024,2,160]{1,3,2,0:T(8,128)(2,1)}, bf16[2,1024,2,160]{1,3,2,0:T(8,128)(2,1)}, bf...) while((s32[]{:T(128)}, ...), condition=%wide.region_15.16_spmd, body=%wide.region_13.15_spmd.sunk | while | flops 3381196800 | bytes 147121552 | solution.py:156
  1223.5 6.0 multiply_reduce_fusion.11
  1229.6 8.2 multiply_convert_fusion.3
  1237.8 6.0 fusion.171
  1250.9 6.0 multiply_reduce_fusion.11
  1257.0 8.2 multiply_convert_fusion.3
  1265.2 6.0 fusion.171
  1289.1 9.0 add_add_fusion.3
  1299.5 5.7 fusion.97
  1308.5 5.7 fusion.92
  1314.2 5.7 fusion.96
  1328.3 327.4 %all-reduce.10.cloned.1.call-done = f32[2048,1280]{1,0:T(8,128)} async-done(((f32[2048,1280]{1,0:T(8,128)}), f32[2048,1280]{1,0:T(8,128)}) %all-reduce.10.cloned.1.call-update) | async-done | bytes 10485776 | tf_op jit(solution)/shard_map/psum | solution.py:171
  1655.7 7.9 fusion.82
  1663.7 9.8 fusion.65
  1673.7 12.9 convert_reduce_fusion.1
  1686.5 26.9 %all-reduce = (f32[1280]{0:T(1024)}, f32[1280]{0:T(1024)}, f32[320]{0:T(512)}, f32[320]{0:T(512)}, f32[1280]{0:T(1024)}, /*index=5*/f32[1280]{0:T(1024)}, f32[1280]{0:T(1024)}, f32[320]{0:T(512)}, f32[1280]{0:T(1024)}) all-reduce(f32[1280]{0:T(1024)S(1)} %get-tuple-element.187, ...), channel_id=1, replica_groups=mesh['dp'=8,'tensor'=4] {'dp'}, use_global_device_ids=true, to_apply=%region_20.21 | all-reduce | flops 8640 | bytes 69120 | tf_op jit(solution)/shard_map/psum | solution.py:191
  1713.5 92.8 %all-reduce.12.cloned.1.call-done = (f32[1280,320]{0,1:T(8,128)}, f32[1280,320]{0,1:T(8,128)}, f32[1280,320]{0,1:T(8,128)}, f32[320,1280]{1,0:T(8,128)}, f32[1280,320]{0,1:T(8,128)}, /*index=5*/f32[320,1280]{1,0:T(8,128)}) async-done(((f32[1280,320]{0,1:T(8,128)}, f32[1280,320]{0,1:T(8,128)}, f32[1280,320]{0,1:T(8,128)}, f32[320,1280]{1,0:T(8,128)}, f32[1280,320]{0,1:T(8,128)}, ...) | async-done | bytes 9830416 | tf_op jit(solution)/shard_map/psum | solution.py:191
  (314 shorter events, 157.6 us)
Async XLA Ops:
  7.2 450.7 %copy-start = (bf16[320,1280]{1,0:T(8,128)(2,1)S(1)}, bf16[320,1280]{1,0:T(8,128)(2,1)}, u32[]{:S(2)}) copy-start(bf16[320,1280]{1,0:T(8,128)(2,1)} %param.37) | copy-start | bytes 2457604
  7.2 427.1 %all-reduce.8.cloned.1.call-start = ((), (), s32[]{:S(2)}) async-start(), calls=%async_computation | async-start | bytes 20971520 | tf_op jit(solution)/shard_map/psum | solution.py:120
  72.9 361.3 %copy-start.69 = (f32[1280]{0:T(1024)S(1)}, f32[1280]{0:T(1024)}, u32[]{:S(2)}) copy-start(f32[1280]{0:T(1024)} %param.32) | copy-start | bytes 15364
  73.0 1106.0 %all-reduce.14.cloned.1.call-start = ((), (), s32[]{:S(2)}) async-start(), calls=%async_computation.3 | async-start | bytes 41943040 | tf_op jit(solution)/shard_map/psum | solution.py:128
  481.0 697.9 %copy-start.71 = (f32[1280]{0:T(1024)S(1)}, f32[1280]{0:T(1024)}, u32[]{:S(2)}) copy-start(f32[1280]{0:T(1024)} %param.38) | copy-start | bytes 15364
  481.1 1174.7 %all-reduce.10.cloned.1.call-start = ((), (), s32[]{:S(2)}) async-start(), calls=%async_computation.1 | async-start | bytes 20971520 | tf_op jit(solution)/shard_map/psum | solution.py:171
  1178.9 15.8 slice-start
  1178.9 15.8 slice-start.8
  1178.9 15.8 slice-start.1
  1178.9 16.2 slice-start.2
  1179.0 17.4 slice-start.9
  1179.0 18.0 slice-start.10
  1298.2 508.1 %all-reduce.12.cloned.1.call-start = ((), (), s32[]{:S(2)}) async-start(), calls=%async_computation.2 | async-start | bytes 19660800 | tf_op jit(solution)/shard_map/psum | solution.py:191
  1308.5 11.4 slice-start.15
  1326.0 329.7 %copy-start.51 = (f32[2048]{0:T(1024)S(1)}, f32[2048]{0:T(1024)}, u32[]{:S(2)}) copy-start(f32[2048]{0:T(1024)} %copy-done.50) | copy-start | bytes 24580
  1326.0 329.7 %copy-start.54 = (f32[1280]{0:T(1024)S(1)}, f32[1280]{0:T(1024)}, u32[]{:S(2)}) copy-start(f32[1280]{0:T(1024)} %param.24) | copy-start | bytes 15364
  1328.3 335.3 %copy-start.61 = (f32[2048]{0:T(1024)S(1)}, f32[2048]{0:T(1024)}, u32[]{:S(2)}) copy-start(f32[2048]{0:T(1024)} %copy-done.60) | copy-start | bytes 24580
  1328.3 335.4 %copy-start.56 = (f32[2048]{0:T(1024)S(1)}, f32[2048]{0:T(1024)}, u32[]{:S(2)}) copy-start(f32[2048]{0:T(1024)} %copy-done.55) | copy-start | bytes 24580
  1655.7 17.8 slice-start.5
  1655.7 17.8 slice-start.6
  1673.6 12.9 copy-start.62
  1673.6 12.9 copy-start.63
  1673.6 12.9 copy-start.64
  1673.7 12.9 copy-start.73
  (85 other events, 324.7 us)
Sparse Core Ops, SparseCore 0:
  73.1 361.1 all-reduce.7
  481.2 697.6 all-reduce.13
  1298.3 357.3 all-reduce.9
  1662.1 144.1 all-reduce.11
where the time goes:
time: 1830 us; the launch traced here: 1820 us
  waiting for transfers between devices  1480 us (81%)
  matrix products  130 us (7%)
  other arithmetic  109 us (6%)
  local copies, waits for them, and re-layouts  60.1 us (3%)
  blocking collectives  26.9 us (1%)
    psum x1, waiting for transfers between devices, shards(): lax.psum(jnp.dot(act, proj_weight, preferred_element_type=jnp.float32), '...  698 us
    psum x1, waiting for transfers between devices, shards(): lax.psum(jnp.dot(mixed, out_weight, preferred_element_type=jnp.float32),...  361 us
    psum x1, waiting for transfers between devices, shards(): d_normed1 = lax.psum(partial_in, 'tensor')  327 us
    psum x1, waiting for transfers between devices, shards(): lax.psum((grad_g1, grad_c1, grad_wq, grad_bq, grad_wk, grad_wv, grad_bv,...  92.8 us
  transfers between devices with their start and end apart: 4, of which 4 were waited for; matrix products, arithmetic and copies ran while one was open for 3% of the time, Pallas kernels for 0%

commit v1 on v0

--- a/solution.py
+++ b/solution.py
@@ -3,6 +3,7 @@
 import jax.numpy as jnp
 from jax import lax
 from jax.sharding import PartitionSpec as P
+from jax.lax import all_gather
 
 HEAD_DIM = 160
 EPS = 1e-05
@@ -117,7 +118,10 @@
     )
     mixed = mixed.reshape(tok_rows, local_heads * HEAD_DIM)
     attended = (
-        lax.psum(jnp.dot(mixed, out_weight, preferred_element_type=jnp.float32), "tensor")
+        jnp.sum(
+            all_gather(jnp.dot(mixed, out_weight, preferred_element_type=jnp.float32), "tensor"),
+            axis=0,
+        )
         + out_bias
     )
     resid = inputs + attended

time: 1830 us -> 2190 us (1.20)
  waiting for transfers between devices: 1480 us -> 1820 us
    all_gather x0 -> x1, waiting for transfers between devices: none -> 703 us  [shards(): all_gather(jnp.dot(mixed, out_weight, preferred_element_type=jnp.float32)...]
    psum x1 -> x0, waiting for transfers between devices: 361 us -> none  [shards(): lax.psum(jnp.dot(mixed, out_weight, preferred_element_type=jnp.float32),...]
where the time goes in v1:
time: 2190 us; the launch traced here: 2180 us
  waiting for transfers between devices  1820 us (83%)
  other arithmetic  130 us (6%)
  matrix products  130 us (6%)
  local copies, waits for them, and re-layouts  59.8 us (3%)
  blocking collectives  26.9 us (1%)
    all_gather x1, waiting for transfers between devices, shards(): all_gather(jnp.dot(mixed, out_weight, preferred_element_type=jnp.float32)...  703 us
    psum x1, waiting for transfers between devices, shards(): lax.psum(jnp.dot(act, proj_weight, preferred_element_type=jnp.float32), '...  697 us
    psum x1, waiting for transfers between devices, shards(): d_normed1 = lax.psum(partial_in, 'tensor')  327 us
    psum x1, waiting for transfers between devices, shards(): lax.psum((grad_g1, grad_c1, grad_wq, grad_bq, grad_wk, grad_wv, grad_bv,...  92.8 us
  transfers between devices with their start and end apart: 4, of which 4 were waited for; matrix products, arithmetic and copies ran while one was open for 3% of the time, Pallas kernels for 0%

profile of v1, /device:TPU:0, one launch (start us, length us, event | category | flops | bytes accessed | tf_op | source)
XLA Modules:
  0.0 2182.7 jit_solution(1729148789519911559)
XLA Ops:
  41.4 20.7 while.26
  72.9 702.6 %all-gather.3.cloned.1.call-done = f32[8192,1280]{1,0:T(8,128)} async-done(((f32[2048,1280]{1,0:T(8,128)}), f32[8192,1280]{1,0:T(8,128)}) %all-gather.3.cloned.1.call-update) | async-done | bytes 41943056 | tf_op jit(solution)/shard_map/all_gather | solution.py:122
  775.5 20.3 reduce_sum.248
  795.8 11.8 fusion.86
  820.8 10.2 convert_reduce_fusion.3
  842.6 697.0 %all-reduce.11.cloned.1.call-done = (f32[2048,1280]{1,0:T(8,128)}, f32[2048,1280]{1,0:T(8,128)}) async-done(((f32[2048,1280]{1,0:T(8,128)}, f32[2048,1280]{1,0:T(8,128)}), (f32[2048,1280]{1,0:T(8,128)}, f32[2048,1280]{1,0:T(8,128)})) %all-reduce.11.cloned.1.call-update) | async-done | bytes 20971536 | tf_op jit(solution)/shard_map/psum | solution.py:132
  1539.7 15.9 multiply_reduce_fusion.2
  1561.5 7.7 convert_reduce_fusion.2
  1580.7 55.4 %while.27 = (s32[]{:T(128)}, bf16[2,1024,2,160]{1,3,2,0:T(8,128)(2,1)}, bf16[2,1024,2,160]{1,3,2,0:T(8,128)(2,1)}, bf16[2,1024,2,160]{1,3,2,0:T(8,128)(2,1)}, bf...) while((s32[]{:T(128)}, ...), condition=%wide.region_15.16_spmd, body=%wide.region_13.15_spmd.sunk | while | flops 3381196800 | bytes 147121552 | solution.py:160
  1584.5 6.0 multiply_reduce_fusion.11
  1590.5 8.2 multiply_convert_fusion.3
  1598.8 6.0 fusion.171
  1611.9 6.0 multiply_reduce_fusion.11
  1617.9 8.2 multiply_convert_fusion.3
  1626.2 6.0 fusion.171
  1649.8 9.1 add_add_fusion.3
  1660.2 5.7 fusion.97
  1674.9 5.7 fusion.96
  1689.1 327.4 %all-reduce.7.cloned.1.call-done = f32[2048,1280]{1,0:T(8,128)} async-done(((f32[2048,1280]{1,0:T(8,128)}), f32[2048,1280]{1,0:T(8,128)}) %all-reduce.7.cloned.1.call-update) | async-done | bytes 10485776 | tf_op jit(solution)/shard_map/psum | solution.py:175
  2016.5 7.9 fusion.82
  2024.5 9.8 fusion.65
  2034.5 12.9 convert_reduce_fusion.1
  2047.4 26.9 %all-reduce = (f32[1280]{0:T(1024)}, f32[1280]{0:T(1024)}, f32[320]{0:T(512)}, f32[320]{0:T(512)}, f32[1280]{0:T(1024)}, /*index=5*/f32[1280]{0:T(1024)}, f32[1280]{0:T(1024)}, f32[320]{0:T(512)}, f32[1280]{0:T(1024)}) all-reduce(f32[1280]{0:T(1024)S(1)} %get-tuple-element.187, ...), channel_id=1, replica_groups=mesh['dp'=8,'tensor'=4] {'dp'}, use_global_device_ids=true, to_apply=%region_20.21 | all-reduce | flops 8640 | bytes 69120 | tf_op jit(solution)/shard_map/psum | solution.py:195
  2074.2 92.8 %all-reduce.9.cloned.1.call-done = (f32[1280,320]{0,1:T(8,128)}, f32[1280,320]{0,1:T(8,128)}, f32[1280,320]{0,1:T(8,128)}, f32[320,1280]{1,0:T(8,128)}, f32[1280,320]{0,1:T(8,128)}, /*index=5*/f32[320,1280]{1,0:T(8,128)}) async-done(((f32[1280,320]{0,1:T(8,128)}, f32[1280,320]{0,1:T(8,128)}, f32[1280,320]{0,1:T(8,128)}, f32[320,1280]{1,0:T(8,128)}, f32[1280,320]{0,1:T(8,128)}, ...) | async-done | bytes 9830416 | tf_op jit(solution)/shard_map/psum | solution.py:195
  (315 shorter events, 162.3 us)
Async XLA Ops:
  7.2 812.2 %copy-start = (bf16[320,1280]{1,0:T(8,128)(2,1)S(1)}, bf16[320,1280]{1,0:T(8,128)(2,1)}, u32[]{:S(2)}) copy-start(bf16[320,1280]{1,0:T(8,128)(2,1)} %param.37) | copy-start | bytes 2457604
  7.2 768.3 %all-gather.3.cloned.1.call-start = ((), (), s32[]{:S(2)}) async-start(), calls=%async_computation.1 | async-start | bytes 52428800 | tf_op jit(solution)/shard_map/all_gather | solution.py:122
  72.8 1466.8 %all-reduce.11.cloned.1.call-start = ((), (), s32[]{:S(2)}) async-start(), calls=%async_computation.3 | async-start | bytes 41943040 | tf_op jit(solution)/shard_map/psum | solution.py:132
  775.5 20.3 copy-start.69
  842.6 697.1 %copy-start.71 = (f32[1280]{0:T(1024)S(1)}, f32[1280]{0:T(1024)}, u32[]{:S(2)}) copy-start(f32[1280]{0:T(1024)} %param.38) | copy-start | bytes 15364
  842.6 1173.9 %all-reduce.7.cloned.1.call-start = ((), (), s32[]{:S(2)}) async-start(), calls=%async_computation | async-start | bytes 20971520 | tf_op jit(solution)/shard_map/psum | solution.py:175
  1539.6 16.0 slice-start
  1539.6 16.0 slice-start.8
  1539.6 16.0 slice-start.1
  1539.6 16.2 slice-start.2
  1539.7 17.4 slice-start.9
  1539.7 18.0 slice-start.10
  1658.9 508.1 %all-reduce.9.cloned.1.call-start = ((), (), s32[]{:S(2)}) async-start(), calls=%async_computation.2 | async-start | bytes 19660800 | tf_op jit(solution)/shard_map/psum | solution.py:195
  1669.3 11.4 slice-start.15
  1686.8 329.7 %copy-start.51 = (f32[2048]{0:T(1024)S(1)}, f32[2048]{0:T(1024)}, u32[]{:S(2)}) copy-start(f32[2048]{0:T(1024)} %copy-done.50) | copy-start | bytes 24580
  1686.8 329.7 %copy-start.54 = (f32[1280]{0:T(1024)S(1)}, f32[1280]{0:T(1024)}, u32[]{:S(2)}) copy-start(f32[1280]{0:T(1024)} %param.24) | copy-start | bytes 15364
  1689.1 335.3 %copy-start.61 = (f32[2048]{0:T(1024)S(1)}, f32[2048]{0:T(1024)}, u32[]{:S(2)}) copy-start(f32[2048]{0:T(1024)} %copy-done.60) | copy-start | bytes 24580
  1689.1 335.4 %copy-start.56 = (f32[2048]{0:T(1024)S(1)}, f32[2048]{0:T(1024)}, u32[]{:S(2)}) copy-start(f32[2048]{0:T(1024)} %copy-done.55) | copy-start | bytes 24580
  2016.5 17.9 slice-start.5
  2016.5 17.9 slice-start.6
  2034.4 12.9 copy-start.62
  2034.4 12.9 copy-start.63
  2034.4 12.9 copy-start.64
  2034.5 12.9 copy-start.73
  (85 other events, 324.8 us)
Sparse Core Ops, SparseCore 0:
  73.0 702.4 all-gather.2
  842.7 696.8 all-reduce.10
  1659.1 357.3 all-reduce.6
  2022.8 144.1 all-reduce.8
